TPU v7x, 32 devices: a whole 2x2x4 slice. The times are simulated.
32 devices in a mesh: leaf: 8 (over y, x, core), panel: 4 (over z).
Axes of the slice: x: 2, y: 2, z: 4, core: 2. Of those that a mesh axis runs over, the one named last changes fastest.
Arguments:
- live_tiles: int32 [15], replicated, may hold values from 8 to 16
- row_tiles: int32 [14, 8], replicated, may hold values from 0 to 47, as said below
- rhs0: float32 [256, 16384], P('panel', 'leaf'), may hold values from -6 to 6
- rhs1: float32 [256, 8192], P('panel', 'leaf'), may hold values from -6 to 6
- rhs2: float32 [256, 4096], P('panel', 'leaf'), may hold values from -6 to 6
- rhs3: float32 [256, 2048], P('panel', 'leaf'), may hold values from -6 to 6
- dinv0: float32 [16384, 2048], P('leaf', 'panel'), as said below
- dinv1: float32 [8192, 2048], P('leaf', 'panel'), as said below
- dinv2: float32 [4096, 2048], P('leaf', 'panel'), as said below
- dinv3: float32 [2048, 2048], P('leaf', 'panel'), as said below
- off0: float32 [8192, 2048], P('leaf', 'panel'), may hold values from -0.125 to 0.125
- off1: float32 [4096, 2048], P('leaf', 'panel'), may hold values from -0.125 to 0.125
- off2: float32 [2048, 2048], P('leaf', 'panel'), may hold values from -0.125 to 0.125
Outputs:
- sol0: float32 [256, 16384], P('panel', 'leaf')
- sol1: float32 [256, 8192], P('panel', 'leaf')
- sol2: float32 [256, 4096], P('panel', 'leaf')
- sol3: float32 [256, 2048], P('panel', 'leaf')
Inputs may be any that keep to these rules, and one draw needn't show every extreme that they name: `row_tiles`: each row names 8 different tiles; for a supernode of level k every value is below (3 - k) * 16. `live_tiles`: counted level by level in the supernodes' order. `dinv0`: each 2048 x 2048 row block is lower triangular with diagonal entries from 0.5 to 2. `dinv1`: each 2048 x 2048 row block is lower triangular with diagonal entries from 0.5 to 2. `dinv2`: each 2048 x 2048 row block is lower triangular with diagonal entries from 0.5 to 2. `dinv3`: each 2048 x 2048 row block is lower triangular with diagonal entries from 0.5 to 2.
All inputs are finite; a program needn't handle non-finite values.
Results may differ from a plain program's by a relative error of at most 0.00028.
Values sent between devices are 32-bit elements; how exact they have to be, the bound alone decides.
A program may use at most 64 MiB of HBM per device.

v0:
```python
import jax
import jax.numpy as jnp
from jax import lax
from jax.sharding import PartitionSpec as P

B = 128
LEVELS = 4
highest = lax.Precision.HIGHEST


def swapped(block, axis, bit):
    count = lax.axis_size(axis)
    route = []
    for low in range(count):
        high = low | 1 << bit
        if high != low and high < count:
            route += [(low, high), (high, low)]
    return lax.ppermute(block, axis, route)


def leaf_bit(leaf_index, bit_number):
    return leaf_index // 2**bit_number % 2


def group_rows(vector, height, leaf_index):
    for bit_number in range(height):
        partner = swapped(vector, "leaf", bit_number)
        is_lower = leaf_bit(leaf_index, bit_number) == 0
        vector = jnp.where(
            is_lower, jnp.concatenate([vector, partner], 1), jnp.concatenate([partner, vector], 1)
        )
    return vector


def group_halving(buffer, height, leaf_index):
    for bit_number in reversed(range(height)):
        half_width = buffer.shape[1] // 2
        is_lower = leaf_bit(leaf_index, bit_number) == 0
        kept_half = jnp.where(is_lower, buffer[:, :half_width], buffer[:, half_width:])
        given_half = jnp.where(is_lower, buffer[:, half_width:], buffer[:, :half_width])
        buffer = kept_half + swapped(given_half, "leaf", bit_number)
    return buffer


def group_total(partial_sum, height):
    for bit_number in range(height):
        partial_sum = partial_sum + swapped(partial_sum, "leaf", bit_number)
    return partial_sum


def to_columns(vector, height, leaf_index):
    full_rows = group_rows(vector, height, leaf_index)
    return lax.all_to_all(full_rows, "panel", split_axis=1, concat_axis=0, tiled=True)


def contract_last(left, right):
    return lax.dot_general(
        left, right, (((1,), (1,)), ((), ())), precision=highest, preferred_element_type=jnp.float32
    )


def selector(chosen, offset, tile_count):
    return (chosen[:, None] == offset + jnp.arange(tile_count, dtype=jnp.int32)[None, :]).astype(
        jnp.float32
    )


def geometry(height, leaf_index, live_tiles, first_node, order_rows):
    group_width = 2**height
    node_index = leaf_index // group_width
    group_place = leaf_index % group_width
    rows_here = order_rows // group_width
    live_count = lax.dynamic_index_in_dim(live_tiles, first_node + node_index, keepdims=False)
    node_mask = (jnp.arange(order_rows, dtype=jnp.int32) < live_count * B).astype(jnp.float32)
    local_mask = lax.dynamic_slice_in_dim(node_mask, group_place * rows_here, rows_here)
    return (node_index, group_place, rows_here, node_mask, local_mask)


def chosen_tiles(row_tiles, first_node, node_index, group_place, local_tiles):
    entry = lax.dynamic_index_in_dim(row_tiles, first_node + node_index, keepdims=False)
    return lax.dynamic_slice_in_dim(entry, group_place * local_tiles, local_tiles)


def local(
    live_tiles, row_tiles, rhs0, rhs1, rhs2, rhs3, dinv0, dinv1, dinv2, dinv3, off0, off1, off2
):
    right_sides = [rhs0, rhs1, rhs2, rhs3]
    inverses = [dinv0, dinv1, dinv2, dinv3]
    off_rows = [off0, off1, off2]
    leaf_index = lax.axis_index("leaf")
    panel_index = lax.axis_index("panel")
    leaf_count = lax.axis_size("leaf")
    panel_count = lax.axis_size("panel")
    order_rows = dinv0.shape[0]
    tile_count = order_rows // B
    share_rows = rhs0.shape[0]
    all_rhs = share_rows * panel_count
    off_tiles = row_tiles.shape[1]
    first_nodes = []
    start_node = 0
    for height in range(LEVELS):
        first_nodes.append(start_node)
        start_node = start_node + leaf_count // 2**height
    buffers = [jnp.zeros((share_rows, order_rows), jnp.float32) for height in range(LEVELS)]
    columns_kept = []
    for height in range(LEVELS):
        node_index, group_place, rows_here, node_mask, local_mask = geometry(
            height, leaf_index, live_tiles, first_nodes[height], order_rows
        )
        residual = right_sides[height]
        if height > 0:
            residual = residual - group_halving(buffers[height], height, leaf_index)
        spread = to_columns(residual * local_mask[None, :], height, leaf_index)
        inverse = inverses[height]
        solved = lax.psum_scatter(
            contract_last(spread, inverse), "panel", scatter_dimension=0, tiled=True
        )
        columns = to_columns(solved * local_mask[None, :], height, leaf_index)
        columns_kept.append(columns)
        if height < LEVELS - 1:
            block_rows = off_rows[height]
            update = lax.psum_scatter(
                contract_last(columns, block_rows), "panel", scatter_dimension=0, tiled=True
            )
            local_tiles = off_tiles // 2**height
            chosen = chosen_tiles(
                row_tiles, first_nodes[height], node_index, group_place, local_tiles
            )
            pieces = update.reshape(share_rows, local_tiles, B)
            for ancestor in range(height + 1, LEVELS):
                picked = selector(chosen, (ancestor - height - 1) * tile_count, tile_count)
                sent = jnp.einsum("rtb,tc->rcb", pieces, picked, precision=highest)
                buffers[ancestor] = buffers[ancestor] + sent.reshape(share_rows, order_rows)
    full_solutions = [None] * LEVELS
    outputs = [None] * LEVELS
    for height in reversed(range(LEVELS)):
        node_index, group_place, rows_here, node_mask, local_mask = geometry(
            height, leaf_index, live_tiles, first_nodes[height], order_rows
        )
        target = columns_kept[height]
        if height < LEVELS - 1:
            local_tiles = off_tiles // 2**height
            chosen = chosen_tiles(
                row_tiles, first_nodes[height], node_index, group_place, local_tiles
            )
            gathered = jnp.zeros((all_rhs, local_tiles, B), jnp.float32)
            for ancestor in range(height + 1, LEVELS):
                picked = selector(chosen, (ancestor - height - 1) * tile_count, tile_count)
                above = full_solutions[ancestor].reshape(all_rhs, tile_count, B)
                gathered = gathered + jnp.einsum("rcb,tc->rtb", above, picked, precision=highest)
            correction = jnp.dot(
                gathered.reshape(all_rhs, local_tiles * B),
                off_rows[height],
                precision=highest,
                preferred_element_type=jnp.float32,
            )
            target = target - group_total(correction, height)
        whole_target = lax.all_gather(target, "panel", axis=1, tiled=True) * node_mask[None, :]
        mine = lax.dynamic_slice_in_dim(whole_target, group_place * rows_here, rows_here, 1)
        partial_sum = jnp.dot(
            mine, inverses[height], precision=highest, preferred_element_type=jnp.float32
        )
        partial_sum = group_total(partial_sum, height)
        whole_solution = (
            lax.all_gather(partial_sum, "panel", axis=1, tiled=True) * node_mask[None, :]
        )
        full_solutions[height] = whole_solution
        outputs[height] = lax.dynamic_slice(
            whole_solution,
            (panel_index * share_rows, group_place * rows_here),
            (share_rows, rows_here),
        )
    return tuple(outputs)


def solution(mesh):
    return jax.shard_map(
        local,
        mesh=mesh,
        in_specs=(
            P(),
            P(),
            P("panel", "leaf"),
            P("panel", "leaf"),
            P("panel", "leaf"),
            P("panel", "leaf"),
            P("leaf", "panel"),
            P("leaf", "panel"),
            P("leaf", "panel"),
            P("leaf", "panel"),
            P("leaf", "panel"),
            P("leaf", "panel"),
            P("leaf", "panel"),
        ),
        out_specs=(P("panel", "leaf"), P("panel", "leaf"), P("panel", "leaf"), P("panel", "leaf")),
        check_vma=False,
    )
```

profile of v0, /device:TPU:0, one launch (start us, length us, event | category | flops | bytes accessed | tf_op | source)
XLA Modules:
  0.0 909.9 jit_solution(4213799960495342376)
XLA Ops:
  10.6 20.6 %all_to_all.134 = f32[64,4,512]{2,0,1:T(8,128)S(1)} all-to-all(f32[64,4,512]{2,0,1:T(8,128)S(1)} %bitcast.207), channel_id=1, replica_groups=mesh['leaf'=8,'panel'=4] {'panel'}, dimensions={1} | all-to-all | bytes 1048576 | tf_op jit(solution)/shard_map/all_to_all | solution.py:53
  31.2 7.1 fusion.71
  38.4 42.8 %reduce-scatter.8.cloned.1.call-done = f32[64,2048]{1,0:T(8,128)} async-done(((f32[256,2048]{1,0:T(8,128)}), f32[64,2048]{1,0:T(8,128)}) %reduce-scatter.8.cloned.1.call-update) | async-done | bytes 524304 | tf_op jit(solution)/shard_map/reduce_scatter | solution.py:115
  82.5 17.5 %all_to_all.135 = f32[64,4,512]{2,0,1:T(8,128)S(1)} all-to-all(f32[64,4,512]{2,0,1:T(8,128)S(1)} %bitcast.209), channel_id=1, replica_groups=mesh['leaf'=8,'panel'=4] {'panel'}, dimensions={1} | all-to-all | bytes 1048576 | tf_op jit(solution)/shard_map/all_to_all | solution.py:53
  103.2 25.9 %reduce-scatter.10.cloned.1.call-done = f32[64,1024]{1,0:T(8,128)} async-done(((f32[256,1024]{1,0:T(8,128)}), f32[64,1024]{1,0:T(8,128)}) %reduce-scatter.10.cloned.1.call-update) | async-done | bytes 262160 | tf_op jit(solution)/shard_map/reduce_scatter | solution.py:122
  136.2 17.5 %all_to_all.136 = f32[64,4,512]{2,0,1:T(8,128)S(1)} all-to-all(f32[64,4,512]{2,0,1:T(8,128)S(1)} %maximum_select_fusion), channel_id=1, replica_groups=mesh['leaf'=8,'panel'=4] {'panel'}, dimensions={1} | all-to-all | bytes 1048576 | tf_op jit(solution)/shard_map/all_to_all | solution.py:53
  156.7 26.4 %reduce-scatter.12.cloned.1.call-done = f32[64,1024]{1,0:T(8,128)} async-done(((f32[256,1024]{1,0:T(8,128)}), f32[64,1024]{1,0:T(8,128)}) %reduce-scatter.12.cloned.1.call-update) | async-done | bytes 262160 | tf_op jit(solution)/shard_map/reduce_scatter | solution.py:115
  185.8 17.5 %all_to_all.137 = f32[64,4,512]{2,0,1:T(8,128)S(1)} all-to-all(f32[64,4,512]{2,0,1:T(8,128)S(1)} %maximum_select_fusion.1), channel_id=1, replica_groups=mesh['leaf'=8,'panel'=4] {'panel'}, dimensions={1} | all-to-all | bytes 1048576 | tf_op jit(solution)/shard_map/all_to_all | solution.py:53
  207.8 19.2 %reduce-scatter.14.cloned.1.call-done = f32[64,512]{1,0:T(8,128)} async-done(((f32[256,512]{1,0:T(8,128)}), f32[64,512]{1,0:T(8,128)}) %reduce-scatter.14.cloned.1.call-update) | async-done | bytes 131088 | tf_op jit(solution)/shard_map/reduce_scatter | solution.py:122
  241.3 6.9 collective-permute-done.6
  248.3 16.7 %all_to_all.138 = f32[64,4,512]{2,0,1:T(8,128)S(1)} all-to-all(f32[64,4,512]{2,0,1:T(8,128)S(1)} %maximum_select_fusion.2), channel_id=1, replica_groups=mesh['leaf'=8,'panel'=4] {'panel'}, dimensions={1} | all-to-all | bytes 1048576 | tf_op jit(solution)/shard_map/all_to_all | solution.py:53
  267.0 20.9 %reduce-scatter.16.cloned.1.call-done = f32[64,512]{1,0:T(8,128)} async-done(((f32[256,512]{1,0:T(8,128)}), f32[64,512]{1,0:T(8,128)}) %reduce-scatter.16.cloned.1.call-update) | async-done | bytes 131088 | tf_op jit(solution)/shard_map/reduce_scatter | solution.py:115
  292.7 6.0 collective-permute-done.8
  298.8 16.6 %all_to_all.139 = f32[64,4,512]{2,0,1:T(8,128)S(1)} all-to-all(f32[64,4,512]{2,0,1:T(8,128)S(1)} %maximum_select_fusion.3), channel_id=1, replica_groups=mesh['leaf'=8,'panel'=4] {'panel'}, dimensions={1} | all-to-all | bytes 1048576 | tf_op jit(solution)/shard_map/all_to_all | solution.py:53
  321.7 15.2 %reduce-scatter.18.cloned.1.call-done = f32[64,256]{1,0:T(8,128)} async-done(((f32[256,256]{1,0:T(8,128)}), f32[64,256]{1,0:T(8,128)}) %reduce-scatter.18.cloned.1.call-update) | async-done | bytes 65552 | tf_op jit(solution)/shard_map/reduce_scatter | solution.py:122
  363.9 6.0 collective-permute-done.14
  370.0 15.8 %all_to_all.140 = f32[64,4,512]{2,0,1:T(8,128)S(1)} all-to-all(f32[64,4,512]{2,0,1:T(8,128)S(1)} %maximum_select_fusion.4), channel_id=1, replica_groups=mesh['leaf'=8,'panel'=4] {'panel'}, dimensions={1} | all-to-all | bytes 1048576 | tf_op jit(solution)/shard_map/all_to_all | solution.py:53
  387.1 19.2 %reduce-scatter.20.cloned.1.call-done = f32[64,256]{1,0:T(8,128)} async-done(((f32[256,256]{1,0:T(8,128)}), f32[64,256]{1,0:T(8,128)}) %reduce-scatter.20.cloned.1.call-update) | async-done | bytes 65552 | tf_op jit(solution)/shard_map/reduce_scatter | solution.py:115
  421.7 16.5 %all_to_all.141 = f32[64,4,512]{2,0,1:T(8,128)} all-to-all(f32[64,4,512]{2,0,1:T(8,128)S(1)} %maximum_select_fusion.5), channel_id=1, replica_groups=mesh['leaf'=8,'panel'=4] {'panel'}, dimensions={1} | all-to-all | bytes 1048576 | tf_op jit(solution)/shard_map/all_to_all | solution.py:53
  438.3 44.8 %all-gather.9.cloned.1.call-done = f32[256,2048]{1,0:T(8,128)} async-done(((f32[256,512]{1,0:T(8,128)}), f32[256,2048]{1,0:T(8,128)}) %all-gather.9.cloned.1.call-update) | async-done | bytes 2097168 | tf_op jit(solution)/shard_map/all_gather | solution.py:158
  488.4 12.5 %collective-permute-done.19 = f32[256,512]{1,0:T(8,128)S(1)} collective-permute-done((f32[256,512]{1,0:T(8,128)S(1)}, f32[256,512]{1,0:T(8,128)S(1)}, u32[]{:S(2)}, u32[]{:S(2)}) %collective-permute-start.19) | collective-permute-done | bytes 524320 | tf_op jit(solution)/shard_map/ppermute | solution.py:18
  502.5 11.6 %collective-permute-done.20 = f32[256,512]{1,0:T(8,128)S(1)} collective-permute-done((f32[256,512]{1,0:T(8,128)S(1)}, f32[256,512]{1,0:T(8,128)S(1)}, u32[]{:S(2)}, u32[]{:S(2)}) %collective-permute-start.20) | collective-permute-done | bytes 524320 | tf_op jit(solution)/shard_map/ppermute | solution.py:18
  515.1 44.6 %all-gather.11.cloned.1.call-done = f32[256,2048]{1,0:T(8,128)} async-done(((f32[256,512]{1,0:T(8,128)}), f32[256,2048]{1,0:T(8,128)}) %all-gather.11.cloned.1.call-update) | async-done | bytes 2097168 | tf_op jit(solution)/shard_map/all_gather | solution.py:165
  567.6 12.5 %collective-permute-done.22 = f32[256,512]{1,0:T(8,128)S(1)} collective-permute-done((f32[256,512]{1,0:T(8,128)S(1)}, f32[256,512]{1,0:T(8,128)S(1)}, u32[]{:S(2)}, u32[]{:S(2)}) %collective-permute-start.22) | collective-permute-done | bytes 524320 | tf_op jit(solution)/shard_map/ppermute | solution.py:18
  581.3 44.4 %all-gather.13.cloned.1.call-done = f32[256,2048]{1,0:T(8,128)} async-done(((f32[256,512]{1,0:T(8,128)}), f32[256,2048]{1,0:T(8,128)}) %all-gather.13.cloned.1.call-update) | async-done | bytes 2097168 | tf_op jit(solution)/shard_map/all_gather | solution.py:158
  631.7 12.5 %collective-permute-done.24 = f32[256,512]{1,0:T(8,128)S(1)} collective-permute-done((f32[256,512]{1,0:T(8,128)S(1)}, f32[256,512]{1,0:T(8,128)S(1)}, u32[]{:S(2)}, u32[]{:S(2)}) %collective-permute-start.24) | collective-permute-done | bytes 524320 | tf_op jit(solution)/shard_map/ppermute | solution.py:18
  645.2 44.6 %all-gather.15.cloned.1.call-done = f32[256,2048]{1,0:T(8,128)} async-done(((f32[256,512]{1,0:T(8,128)}), f32[256,2048]{1,0:T(8,128)}) %all-gather.15.cloned.1.call-update) | async-done | bytes 2097168 | tf_op jit(solution)/shard_map/all_gather | solution.py:165
  699.6 44.6 %all-gather.17.cloned.1.call-done = f32[256,2048]{1,0:T(8,128)} async-done(((f32[256,512]{1,0:T(8,128)}), f32[256,2048]{1,0:T(8,128)}) %all-gather.17.cloned.1.call-update) | async-done | bytes 2097168 | tf_op jit(solution)/shard_map/all_gather | solution.py:158
  750.5 44.4 %all-gather.19.cloned.1.call-done = f32[256,2048]{1,0:T(8,128)} async-done(((f32[256,512]{1,0:T(8,128)}), f32[256,2048]{1,0:T(8,128)}) %all-gather.19.cloned.1.call-update) | async-done | bytes 2097168 | tf_op jit(solution)/shard_map/all_gather | solution.py:165
  804.7 44.6 %all-gather.21.cloned.1.call-done = f32[256,2048]{1,0:T(8,128)} async-done(((f32[256,512]{1,0:T(8,128)}), f32[256,2048]{1,0:T(8,128)}) %all-gather.21.cloned.1.call-update) | async-done | bytes 2097168 | tf_op jit(solution)/shard_map/all_gather | solution.py:158
  849.3 7.3 fusion
  861.9 39.3 %all-gather.23.cloned.1.call-done = f32[256,2048]{1,0:T(8,128)} async-done(((f32[256,512]{1,0:T(8,128)}), f32[256,2048]{1,0:T(8,128)}) %all-gather.23.cloned.1.call-update) | async-done | bytes 2097168 | tf_op jit(solution)/shard_map/all_gather | solution.py:165
  (255 shorter events, 150.3 us)
Async XLA Ops:
  7.2 74.1 %reduce-scatter.8.cloned.1.call-start = ((), (), s32[]{:S(2)}) async-start(), calls=%async_computation.15 | async-start | bytes 2621440 | tf_op jit(solution)/shard_map/reduce_scatter | solution.py:115
  38.4 90.8 %reduce-scatter.10.cloned.1.call-start = ((), (), s32[]{:S(2)}) async-start(), calls=%async_computation.16 | async-start | bytes 1310720 | tf_op jit(solution)/shard_map/reduce_scatter | solution.py:122
  103.0 80.1 %reduce-scatter.12.cloned.1.call-start = ((), (), s32[]{:S(2)}) async-start(), calls=%async_computation.17 | async-start | bytes 1310720 | tf_op jit(solution)/shard_map/reduce_scatter | solution.py:115
  156.6 70.4 %reduce-scatter.14.cloned.1.call-start = ((), (), s32[]{:S(2)}) async-start(), calls=%async_computation.18 | async-start | bytes 655360 | tf_op jit(solution)/shard_map/reduce_scatter | solution.py:122
  206.0 81.9 %reduce-scatter.16.cloned.1.call-start = ((), (), s32[]{:S(2)}) async-start(), calls=%async_computation.19 | async-start | bytes 655360 | tf_op jit(solution)/shard_map/reduce_scatter | solution.py:115
  229.4 6.5 collective-permute-start.3
  239.7 8.5 collective-permute-start.6
  266.9 70.0 %reduce-scatter.18.cloned.1.call-start = ((), (), s32[]{:S(2)}) async-start(), calls=%async_computation.20 | async-start | bytes 327680 | tf_op jit(solution)/shard_map/reduce_scatter | solution.py:122
  290.3 8.4 collective-permute-start.8
  317.8 88.5 %reduce-scatter.20.cloned.1.call-start = ((), (), s32[]{:S(2)}) async-start(), calls=%async_computation.21 | async-start | bytes 327680 | tf_op jit(solution)/shard_map/reduce_scatter | solution.py:115
  340.7 6.4 collective-permute-start.9
  347.9 5.2 collective-permute-start.10
  356.7 5.6 collective-permute-start.13
  362.3 7.6 collective-permute-start.14
  387.1 96.0 %all-gather.9.cloned.1.call-start = ((), (), s32[]{:S(2)}) async-start(), calls=%async_computation.22 | async-start | bytes 2621440 | tf_op jit(solution)/shard_map/all_gather | solution.py:158
  408.4 5.6 collective-permute-start.16
  414.1 7.6 collective-permute-start.17
  438.2 121.5 %all-gather.11.cloned.1.call-start = ((), (), s32[]{:S(2)}) async-start(), calls=%async_computation.23 | async-start | bytes 2621440 | tf_op jit(solution)/shard_map/all_gather | solution.py:165
  484.8 2.0 collective-permute-start.18
  486.9 14.0 %collective-permute-start.19 = (f32[256,512]{1,0:T(8,128)S(1)}, f32[256,512]{1,0:T(8,128)S(1)}, u32[]{:S(2)}, u32[]{:S(2)}) collective-permute-start(f32[256,512]{1,0:T(8,128)S(1)} %add.290), channel_id=1, source_target_pairs={{0,8},{8,0},{4,12},{12,4},{16,24},{24,16},{20,28},{28,20},{1,9},{9... | collective-permute-start | bytes 1572872 | tf_op jit(solution)/shard_map/ppermute | solution.py:18
  501.0 13.2 %collective-permute-start.20 = (f32[256,512]{1,0:T(8,128)S(1)}, f32[256,512]{1,0:T(8,128)S(1)}, u32[]{:S(2)}, u32[]{:S(2)}) collective-permute-start(f32[256,512]{1,0:T(8,128)S(1)} %add.291), channel_id=1, source_target_pairs={{0,16},{16,0},{4,20},{20,4},{8,24},{24,8},{12,28},{28,12},{1,17},{... | collective-permute-start | bytes 1572872 | tf_op jit(solution)/shard_map/ppermute | solution.py:18
  515.1 110.6 %all-gather.13.cloned.1.call-start = ((), (), s32[]{:S(2)}) async-start(), calls=%async_computation.24 | async-start | bytes 2621440 | tf_op jit(solution)/shard_map/all_gather | solution.py:158
  564.0 2.0 collective-permute-start.21
  566.0 14.0 %collective-permute-start.22 = (f32[256,512]{1,0:T(8,128)S(1)}, f32[256,512]{1,0:T(8,128)S(1)}, u32[]{:S(2)}, u32[]{:S(2)}) collective-permute-start(f32[256,512]{1,0:T(8,128)S(1)} %add.293), channel_id=1, source_target_pairs={{0,8},{8,0},{4,12},{12,4},{16,24},{24,16},{20,28},{28,20},{1,9},{9... | collective-permute-start | bytes 1572872 | tf_op jit(solution)/shard_map/ppermute | solution.py:18
  581.0 108.7 %all-gather.15.cloned.1.call-start = ((), (), s32[]{:S(2)}) async-start(), calls=%async_computation.25 | async-start | bytes 2621440 | tf_op jit(solution)/shard_map/all_gather | solution.py:165
  628.1 2.0 collective-permute-start.23
  630.2 14.0 %collective-permute-start.24 = (f32[256,512]{1,0:T(8,128)S(1)}, f32[256,512]{1,0:T(8,128)S(1)}, u32[]{:S(2)}, u32[]{:S(2)}) collective-permute-start(f32[256,512]{1,0:T(8,128)S(1)} %add.295), channel_id=1, source_target_pairs={{0,8},{8,0},{4,12},{12,4},{16,24},{24,16},{20,28},{28,20},{1,9},{9... | collective-permute-start | bytes 1572872 | tf_op jit(solution)/shard_map/ppermute | solution.py:18
  645.1 99.1 %all-gather.17.cloned.1.call-start = ((), (), s32[]{:S(2)}) async-start(), calls=%async_computation.26 | async-start | bytes 2621440 | tf_op jit(solution)/shard_map/all_gather | solution.py:158
  696.6 2.0 collective-permute-start.25
  699.6 95.3 %all-gather.19.cloned.1.call-start = ((), (), s32[]{:S(2)}) async-start(), calls=%async_computation.27 | async-start | bytes 2621440 | tf_op jit(solution)/shard_map/all_gather | solution.py:165
  750.2 99.1 %all-gather.21.cloned.1.call-start = ((), (), s32[]{:S(2)}) async-start(), calls=%async_computation.28 | async-start | bytes 2621440 | tf_op jit(solution)/shard_map/all_gather | solution.py:158
  804.7 96.6 %all-gather.23.cloned.1.call-start = ((), (), s32[]{:S(2)}) async-start(), calls=%async_computation.29 | async-start | bytes 2621440 | tf_op jit(solution)/shard_map/all_gather | solution.py:165
  (43 other events, 666.6 us)
Sparse Core Ops, SparseCore 0:
  38.5 42.7 reduce-scatter.7
  103.1 25.9 reduce-scatter.9
  156.7 26.3 reduce-scatter.11
  206.1 20.8 reduce-scatter.13
  267.0 20.8 reduce-scatter.15
  317.9 18.9 reduce-scatter.17
  387.2 19.0 reduce-scatter.19
  438.3 44.6 all-gather.8
  515.2 44.4 all-gather.10
  581.1 44.4 all-gather.12
  645.2 44.4 all-gather.14
  699.7 44.4 all-gather.16
  750.4 44.4 all-gather.18
  804.8 44.4 all-gather.20
  856.8 44.4 all-gather.22
where the time goes:
time: 919 us; the launch traced here: 910 us
  waiting for transfers between devices  635 us (69%)
  blocking collectives  139 us (15%)
  matrix products  51.3 us (6%)
  other arithmetic  26.6 us (3%)
  starting transfers between devices  22.7 us (2%)
  between operations  17.7 us (2%)
  local copies, waits for them, and re-layouts  17.6 us (2%)
    all_gather x4, waiting for transfers between devices, local(): lax.all_gather(target, 'panel', axis=1, tiled=True) * node_mask[None, :]  178 us
    all_gather x4, waiting for transfers between devices, local(): lax.all_gather(partial_sum, 'panel', axis=1, tiled=True)  173 us
    all_to_all x8, blocking collectives, to_columns(): lax.all_to_all(full_rows, 'panel', split_axis=1, concat_axis=0, tiled=True)  139 us
    ppermute x27, waiting for transfers between devices, swapped(): return lax.ppermute(block, axis, route)  114 us
    reduce_scatter x4, waiting for transfers between devices, local(): lax.psum_scatter(contract_last(spread, inverse), 'panel', scatter_dimensi...  109 us
    reduce_scatter x3, waiting for transfers between devices, local(): lax.psum_scatter(contract_last(columns, block_rows), 'panel', scatter_dim...  60.3 us
    ppermute x27, starting transfers between devices, swapped(): return lax.ppermute(block, axis, route)  21.2 us
    dot_general x7, matrix products, contract_last(): lax.dot_general(left, right, (((1,), (1,)), ((), ())), precision=highest,...  20.4 us
  transfers between devices with their start and end apart: 42, of which 42 were waited for; matrix products, arithmetic and copies ran while one was open for 1% of the time, Pallas kernels for 0%

commit v1 on v0

--- a/solution.py
+++ b/solution.py
@@ -1,3 +1,4 @@
+import functools
 import jax
 import jax.numpy as jnp
 from jax import lax
@@ -6,6 +7,37 @@
 B = 128
 LEVELS = 4
 highest = lax.Precision.HIGHEST
+
+
+def _touch_side(u, in_dim):
+    found_now = list(u.shape[1:])
+    found_now[in_dim] *= u.shape[0]
+    lower = jnp.moveaxis(u, 0, in_dim).reshape(found_now)
+    return lower
+
+
+def frame_push(matrix, chip_axis, axis_k):
+    count_all = jax.lax.axis_size(chip_axis)
+    leaves = [(w, (w + 1) % count_all) for w in range(count_all)]
+    log = [(rr, d) for d, rr in leaves]
+    block_out, piece_now = ([], [])
+    for ix in range(count_all - 1):
+        if ix % 2 == 0:
+            block_out.append(
+                jax.lax.ppermute(block_out[-1] if block_out else matrix, chip_axis, leaves)
+            )
+        else:
+            piece_now.append(
+                jax.lax.ppermute(piece_now[-1] if piece_now else matrix, chip_axis, log)
+            )
+    z1 = jnp.stack([*block_out[::-1], matrix, *piece_now])
+    formed = jax.lax.axis_index(chip_axis) - len(block_out)
+    z1 = z1[(jnp.arange(count_all) - formed) % count_all]
+    item_now = _touch_side(z1, axis_k)
+    return item_now
+
+
+save_array_over_axis = functools.partial(frame_push, chip_axis="panel", axis_k=1)
 
 
 def swapped(block, axis, bit):
@@ -161,9 +193,7 @@
             mine, inverses[height], precision=highest, preferred_element_type=jnp.float32
         )
         partial_sum = group_total(partial_sum, height)
-        whole_solution = (
-            lax.all_gather(partial_sum, "panel", axis=1, tiled=True) * node_mask[None, :]
-        )
+        whole_solution = save_array_over_axis(partial_sum) * node_mask[None, :]
         full_solutions[height] = whole_solution
         outputs[height] = lax.dynamic_slice(
             whole_solution,

time: 919 us -> 941 us (1.024)
  waiting for transfers between devices: 635 us -> 586 us
  local copies, waits for them, and re-layouts: 17.6 us -> 53.2 us
  starting transfers between devices: 22.7 us -> 42.9 us
  other arithmetic: 26.6 us -> 38.3 us
    all_gather x4 -> x0, waiting for transfers between devices: 173 us -> none  [local(): lax.all_gather(partial_sum, 'panel', axis=1, tiled=True)]
    ppermute x0 -> x12, waiting for transfers between devices: none -> 124 us  [the longest x8 103 us: frame_push(): jax.lax.ppermute(block_out[-1] if block_out else matrix, chip_axis, leaves)]
    ppermute x0 -> x12, starting transfers between devices: none -> 20.9 us  [the longest x4 14.6 us: frame_push(): jax.lax.ppermute(piece_now[-1] if piece_now else matrix, chip_axis, log)]
    gather x0 -> x4, local copies, waits for them, and re-layouts: none -> 14.4 us  [frame_push(): z1 = z1[(jnp.arange(count_all) - formed) % count_all]]
    transpose x0 -> x4, local copies, waits for them, and re-layouts: none -> 11.7 us  [_touch_side(): lower = jnp.moveaxis(u, 0, in_dim).reshape(found_now)]
    mul x4 -> x7, other arithmetic: 4.41 us -> 14.2 us  [local(): whole_solution = save_array_over_axis(partial_sum) * node_mask[None, :]]
  transfers between devices with their start and end apart: 42 -> 50, of which waited for: 42 -> 50; matrix products, arithmetic and copies ran while one was open for 1% -> 1% of each run, Pallas kernels for 0% -> 0%
where the time goes in v1:
time: 941 us; the launch traced here: 931 us
  waiting for transfers between devices  586 us (62%)
  blocking collectives  139 us (15%)
  matrix products  55 us (6%)
  local copies, waits for them, and re-layouts  53.2 us (6%)
  starting transfers between devices  42.9 us (5%)
  other arithmetic  38.3 us (4%)
  between operations  17.6 us (2%)
    all_gather x4, waiting for transfers between devices, local(): lax.all_gather(target, 'panel', axis=1, tiled=True) * node_mask[None, :]  177 us
    all_to_all x8, blocking collectives, to_columns(): lax.all_to_all(full_rows, 'panel', split_axis=1, concat_axis=0, tiled=True)  139 us
    ppermute x27, waiting for transfers between devices, swapped(): return lax.ppermute(block, axis, route)  115 us
    reduce_scatter x4, waiting for transfers between devices, local(): lax.psum_scatter(contract_last(spread, inverse), 'panel', scatter_dimensi...  109 us
    ppermute x8, waiting for transfers between devices, frame_push(): jax.lax.ppermute(block_out[-1] if block_out else matrix, chip_axis, leaves)  103 us
    reduce_scatter x3, waiting for transfers between devices, local(): lax.psum_scatter(contract_last(columns, block_rows), 'panel', scatter_dim...  60.7 us
    ppermute x4, waiting for transfers between devices, frame_push(): jax.lax.ppermute(piece_now[-1] if piece_now else matrix, chip_axis, log)  21.4 us
    ppermute x27, starting transfers between devices, swapped(): return lax.ppermute(block, axis, route)  21.1 us
  transfers between devices with their start and end apart: 50, of which 50 were waited for; matrix products, arithmetic and copies ran while one was open for 1% of the time, Pallas kernels for 0%

profile of v1, /device:TPU:0, one launch (start us, length us, event | category | flops | bytes accessed | tf_op | source)
XLA Modules:
  0.0 931.4 jit_solution(82532490219599665)
XLA Ops:
  10.5 20.6 %all_to_all.134 = f32[64,4,512]{2,0,1:T(8,128)S(1)} all-to-all(f32[64,4,512]{2,0,1:T(8,128)S(1)} %bitcast.235), channel_id=1, replica_groups=mesh['leaf'=8,'panel'=4] {'panel'}, dimensions={1} | all-to-all | bytes 1048576 | tf_op jit(solution)/shard_map/all_to_all | solution.py:85
  38.4 42.8 %reduce-scatter.8.cloned.1.call-done = f32[64,2048]{1,0:T(8,128)} async-done(((f32[256,2048]{1,0:T(8,128)}), f32[64,2048]{1,0:T(8,128)}) %reduce-scatter.8.cloned.1.call-update) | async-done | bytes 524304 | tf_op jit(solution)/shard_map/reduce_scatter | solution.py:147
  82.5 17.5 %all_to_all.135 = f32[64,4,512]{2,0,1:T(8,128)S(1)} all-to-all(f32[64,4,512]{2,0,1:T(8,128)S(1)} %bitcast.237), channel_id=1, replica_groups=mesh['leaf'=8,'panel'=4] {'panel'}, dimensions={1} | all-to-all | bytes 1048576 | tf_op jit(solution)/shard_map/all_to_all | solution.py:85
  103.2 25.9 %reduce-scatter.10.cloned.1.call-done = f32[64,1024]{1,0:T(8,128)} async-done(((f32[256,1024]{1,0:T(8,128)}), f32[64,1024]{1,0:T(8,128)}) %reduce-scatter.10.cloned.1.call-update) | async-done | bytes 262160 | tf_op jit(solution)/shard_map/reduce_scatter | solution.py:154
  136.1 17.5 %all_to_all.136 = f32[64,4,512]{2,0,1:T(8,128)S(1)} all-to-all(f32[64,4,512]{2,0,1:T(8,128)S(1)} %maximum_select_fusion), channel_id=1, replica_groups=mesh['leaf'=8,'panel'=4] {'panel'}, dimensions={1} | all-to-all | bytes 1048576 | tf_op jit(solution)/shard_map/all_to_all | solution.py:85
  156.6 26.4 %reduce-scatter.12.cloned.1.call-done = f32[64,1024]{1,0:T(8,128)} async-done(((f32[256,1024]{1,0:T(8,128)}), f32[64,1024]{1,0:T(8,128)}) %reduce-scatter.12.cloned.1.call-update) | async-done | bytes 262160 | tf_op jit(solution)/shard_map/reduce_scatter | solution.py:147
  185.8 17.5 %all_to_all.137 = f32[64,4,512]{2,0,1:T(8,128)S(1)} all-to-all(f32[64,4,512]{2,0,1:T(8,128)S(1)} %maximum_select_fusion.1), channel_id=1, replica_groups=mesh['leaf'=8,'panel'=4] {'panel'}, dimensions={1} | all-to-all | bytes 1048576 | tf_op jit(solution)/shard_map/all_to_all | solution.py:85
  207.2 19.8 %reduce-scatter.14.cloned.1.call-done = f32[64,512]{1,0:T(8,128)} async-done(((f32[256,512]{1,0:T(8,128)}), f32[64,512]{1,0:T(8,128)}) %reduce-scatter.14.cloned.1.call-update) | async-done | bytes 131088 | tf_op jit(solution)/shard_map/reduce_scatter | solution.py:154
  247.7 16.7 %all_to_all.138 = f32[64,4,512]{2,0,1:T(8,128)S(1)} all-to-all(f32[64,4,512]{2,0,1:T(8,128)S(1)} %maximum_select_fusion.2), channel_id=1, replica_groups=mesh['leaf'=8,'panel'=4] {'panel'}, dimensions={1} | all-to-all | bytes 1048576 | tf_op jit(solution)/shard_map/all_to_all | solution.py:85
  266.3 21.0 %reduce-scatter.16.cloned.1.call-done = f32[64,512]{1,0:T(8,128)} async-done(((f32[256,512]{1,0:T(8,128)}), f32[64,512]{1,0:T(8,128)}) %reduce-scatter.16.cloned.1.call-update) | async-done | bytes 131088 | tf_op jit(solution)/shard_map/reduce_scatter | solution.py:147
  298.1 16.6 %all_to_all.139 = f32[64,4,512]{2,0,1:T(8,128)S(1)} all-to-all(f32[64,4,512]{2,0,1:T(8,128)S(1)} %maximum_select_fusion.3), channel_id=1, replica_groups=mesh['leaf'=8,'panel'=4] {'panel'}, dimensions={1} | all-to-all | bytes 1048576 | tf_op jit(solution)/shard_map/all_to_all | solution.py:85
  321.2 15.1 %reduce-scatter.18.cloned.1.call-done = f32[64,256]{1,0:T(8,128)} async-done(((f32[256,256]{1,0:T(8,128)}), f32[64,256]{1,0:T(8,128)}) %reduce-scatter.18.cloned.1.call-update) | async-done | bytes 65552 | tf_op jit(solution)/shard_map/reduce_scatter | solution.py:154
  369.3 15.8 %all_to_all.140 = f32[64,4,512]{2,0,1:T(8,128)S(1)} all-to-all(f32[64,4,512]{2,0,1:T(8,128)S(1)} %maximum_select_fusion.4), channel_id=1, replica_groups=mesh['leaf'=8,'panel'=4] {'panel'}, dimensions={1} | all-to-all | bytes 1048576 | tf_op jit(solution)/shard_map/all_to_all | solution.py:85
  386.5 19.1 %reduce-scatter.20.cloned.1.call-done = f32[64,256]{1,0:T(8,128)} async-done(((f32[256,256]{1,0:T(8,128)}), f32[64,256]{1,0:T(8,128)}) %reduce-scatter.20.cloned.1.call-update) | async-done | bytes 65552 | tf_op jit(solution)/shard_map/reduce_scatter | solution.py:147
  421.0 16.5 %all_to_all.141 = f32[64,4,512]{2,0,1:T(8,128)} all-to-all(f32[64,4,512]{2,0,1:T(8,128)S(1)} %maximum_select_fusion.5), channel_id=1, replica_groups=mesh['leaf'=8,'panel'=4] {'panel'}, dimensions={1} | all-to-all | bytes 1048576 | tf_op jit(solution)/shard_map/all_to_all | solution.py:85
  439.6 44.8 %all-gather.5.cloned.1.call-done = f32[256,2048]{0,1:T(8,128)} async-done(((f32[256,512]{0,1:T(8,128)}), f32[256,2048]{0,1:T(8,128)}) %all-gather.5.cloned.1.call-update) | async-done | bytes 2097168 | tf_op jit(solution)/shard_map/all_gather | solution.py:190
  489.8 12.5 %collective-permute-done.19 = f32[256,512]{1,0:T(8,128)S(1)} collective-permute-done((f32[256,512]{1,0:T(8,128)S(1)}, f32[256,512]{1,0:T(8,128)S(1)}, u32[]{:S(2)}, u32[]{:S(2)}) %collective-permute-start.19) | collective-permute-done | bytes 524320 | tf_op jit(solution)/shard_map/ppermute | solution.py:50
  504.0 11.6 %collective-permute-done.20 = f32[256,512]{1,0:T(8,128)S(1)} collective-permute-done((f32[256,512]{1,0:T(8,128)S(1)}, f32[256,512]{1,0:T(8,128)S(1)}, u32[]{:S(2)}, u32[]{:S(2)}) %collective-permute-start.20) | collective-permute-done | bytes 524320 | tf_op jit(solution)/shard_map/ppermute | solution.py:50
  520.3 13.1 %collective-permute-done.21 = f32[256,512]{1,0:T(8,128)} collective-permute-done((f32[256,512]{1,0:T(8,128)}, f32[256,512]{1,0:T(8,128)}, u32[]{:S(2)}, u32[]{:S(2)}) %collective-permute-start.21) | collective-permute-done | bytes 524320 | tf_op jit(solution)/shard_map/ppermute | solution.py:27
  540.9 12.4 %collective-permute-done.22 = f32[256,512]{1,0:T(8,128)} collective-permute-done((f32[256,512]{1,0:T(8,128)}, f32[256,512]{1,0:T(8,128)}, u32[]{:S(2)}, u32[]{:S(2)}) %collective-permute-start.22) | collective-permute-done | bytes 524320 | tf_op jit(solution)/shard_map/ppermute | solution.py:27
  575.9 12.5 %collective-permute-done.25 = f32[256,512]{1,0:T(8,128)S(1)} collective-permute-done((f32[256,512]{1,0:T(8,128)S(1)}, f32[256,512]{1,0:T(8,128)S(1)}, u32[]{:S(2)}, u32[]{:S(2)}) %collective-permute-start.25) | collective-permute-done | bytes 524320 | tf_op jit(solution)/shard_map/ppermute | solution.py:50
  589.4 43.9 %all-gather.7.cloned.1.call-done = f32[256,2048]{1,0:T(8,128)} async-done(((f32[256,512]{1,0:T(8,128)}), f32[256,2048]{1,0:T(8,128)}) %all-gather.7.cloned.1.call-update) | async-done | bytes 2097168 | tf_op jit(solution)/shard_map/all_gather | solution.py:190
  639.4 12.5 %collective-permute-done.27 = f32[256,512]{1,0:T(8,128)S(1)} collective-permute-done((f32[256,512]{1,0:T(8,128)S(1)}, f32[256,512]{1,0:T(8,128)S(1)}, u32[]{:S(2)}, u32[]{:S(2)}) %collective-permute-start.27) | collective-permute-done | bytes 524320 | tf_op jit(solution)/shard_map/ppermute | solution.py:50
  655.9 12.8 %collective-permute-done.28 = f32[256,512]{1,0:T(8,128)S(1)} collective-permute-done((f32[256,512]{1,0:T(8,128)S(1)}, f32[256,512]{1,0:T(8,128)S(1)}, u32[]{:S(2)}, u32[]{:S(2)}) %collective-permute-start.28) | collective-permute-done | bytes 524320 | tf_op jit(solution)/shard_map/ppermute | solution.py:27
  676.5 13.0 %collective-permute-done.29 = f32[256,512]{1,0:T(8,128)S(1)} collective-permute-done((f32[256,512]{1,0:T(8,128)S(1)}, f32[256,512]{1,0:T(8,128)S(1)}, u32[]{:S(2)}, u32[]{:S(2)}) %collective-permute-start.29) | collective-permute-done | bytes 524320 | tf_op jit(solution)/shard_map/ppermute | solution.py:27
  711.8 43.9 %all-gather.9.cloned.1.call-done = f32[256,2048]{1,0:T(8,128)} async-done(((f32[256,512]{1,0:T(8,128)}), f32[256,2048]{1,0:T(8,128)}) %all-gather.9.cloned.1.call-update) | async-done | bytes 2097168 | tf_op jit(solution)/shard_map/all_gather | solution.py:190
  764.9 12.8 %collective-permute-done.33 = f32[256,512]{1,0:T(8,128)S(1)} collective-permute-done((f32[256,512]{1,0:T(8,128)S(1)}, f32[256,512]{1,0:T(8,128)S(1)}, u32[]{:S(2)}, u32[]{:S(2)}) %collective-permute-start.33) | collective-permute-done | bytes 524320 | tf_op jit(solution)/shard_map/ppermute | solution.py:27
  777.9 8.4 collective-permute-done.35
  786.3 13.0 %collective-permute-done.34 = f32[256,512]{1,0:T(8,128)S(1)} collective-permute-done((f32[256,512]{1,0:T(8,128)S(1)}, f32[256,512]{1,0:T(8,128)S(1)}, u32[]{:S(2)}, u32[]{:S(2)}) %collective-permute-start.34) | collective-permute-done | bytes 524320 | tf_op jit(solution)/shard_map/ppermute | solution.py:27
  822.4 44.0 %all-gather.11.cloned.1.call-done = f32[256,2048]{1,0:T(8,128)} async-done(((f32[256,512]{1,0:T(8,128)}), f32[256,2048]{1,0:T(8,128)}) %all-gather.11.cloned.1.call-update) | async-done | bytes 2097168 | tf_op jit(solution)/shard_map/all_gather | solution.py:190
  876.7 12.8 %collective-permute-done.36 = f32[256,512]{1,0:T(8,128)S(1)} collective-permute-done((f32[256,512]{1,0:T(8,128)S(1)}, f32[256,512]{1,0:T(8,128)S(1)}, u32[]{:S(2)}, u32[]{:S(2)}) %collective-permute-start.36) | collective-permute-done | bytes 524320 | tf_op jit(solution)/shard_map/ppermute | solution.py:27
  897.7 13.0 %collective-permute-done.37 = f32[256,512]{1,0:T(8,128)} collective-permute-done((f32[256,512]{1,0:T(8,128)S(1)}, f32[256,512]{1,0:T(8,128)}, u32[]{:S(2)}, u32[]{:S(2)}) %collective-permute-start.37) | collective-permute-done | bytes 524320 | tf_op jit(solution)/shard_map/ppermute | solution.py:27
  (269 shorter events, 268.0 us)
Async XLA Ops:
  7.2 74.1 %reduce-scatter.8.cloned.1.call-start = ((), (), s32[]{:S(2)}) async-start(), calls=%async_computation.15 | async-start | bytes 2621440 | tf_op jit(solution)/shard_map/reduce_scatter | solution.py:147
  38.3 90.8 %reduce-scatter.10.cloned.1.call-start = ((), (), s32[]{:S(2)}) async-start(), calls=%async_computation.16 | async-start | bytes 1310720 | tf_op jit(solution)/shard_map/reduce_scatter | solution.py:154
  103.0 80.1 %reduce-scatter.12.cloned.1.call-start = ((), (), s32[]{:S(2)}) async-start(), calls=%async_computation.17 | async-start | bytes 1310720 | tf_op jit(solution)/shard_map/reduce_scatter | solution.py:147
  156.6 70.4 %reduce-scatter.14.cloned.1.call-start = ((), (), s32[]{:S(2)}) async-start(), calls=%async_computation.18 | async-start | bytes 655360 | tf_op jit(solution)/shard_map/reduce_scatter | solution.py:154
  205.9 81.3 %reduce-scatter.16.cloned.1.call-start = ((), (), s32[]{:S(2)}) async-start(), calls=%async_computation.19 | async-start | bytes 655360 | tf_op jit(solution)/shard_map/reduce_scatter | solution.py:147
  228.7 6.5 collective-permute-start.3
  239.1 8.5 collective-permute-start.6
  266.2 70.0 %reduce-scatter.18.cloned.1.call-start = ((), (), s32[]{:S(2)}) async-start(), calls=%async_computation.20 | async-start | bytes 327680 | tf_op jit(solution)/shard_map/reduce_scatter | solution.py:154
  289.6 8.4 collective-permute-start.8
  317.1 88.5 %reduce-scatter.20.cloned.1.call-start = ((), (), s32[]{:S(2)}) async-start(), calls=%async_computation.21 | async-start | bytes 327680 | tf_op jit(solution)/shard_map/reduce_scatter | solution.py:147
  361.6 7.6 collective-permute-start.14
  386.4 98.0 %all-gather.5.cloned.1.call-start = ((), (), s32[]{:S(2)}) async-start(), calls=%async_computation.22 | async-start | bytes 2621440 | tf_op jit(solution)/shard_map/all_gather | solution.py:190
  413.4 7.6 collective-permute-start.17
  439.6 193.8 %all-gather.7.cloned.1.call-start = ((), (), s32[]{:S(2)}) async-start(), calls=%async_computation.23 | async-start | bytes 2621440 | tf_op jit(solution)/shard_map/all_gather | solution.py:190
  488.3 14.0 %collective-permute-start.19 = (f32[256,512]{1,0:T(8,128)S(1)}, f32[256,512]{1,0:T(8,128)S(1)}, u32[]{:S(2)}, u32[]{:S(2)}) collective-permute-start(f32[256,512]{1,0:T(8,128)S(1)} %add.326), channel_id=1, source_target_pairs={{0,8},{8,0},{4,12},{12,4},{16,24},{24,16},{20,28},{28,20},{1,9},{9... | collective-permute-start | bytes 1572872 | tf_op jit(solution)/shard_map/ppermute | solution.py:50
  502.4 13.2 %collective-permute-start.20 = (f32[256,512]{1,0:T(8,128)S(1)}, f32[256,512]{1,0:T(8,128)S(1)}, u32[]{:S(2)}, u32[]{:S(2)}) collective-permute-start(f32[256,512]{1,0:T(8,128)S(1)} %add.327), channel_id=1, source_target_pairs={{0,16},{16,0},{4,20},{20,4},{8,24},{24,8},{12,28},{28,12},{1,17},{... | collective-permute-start | bytes 1572872 | tf_op jit(solution)/shard_map/ppermute | solution.py:50
  516.5 16.9 %collective-permute-start.21 = (f32[256,512]{1,0:T(8,128)}, f32[256,512]{1,0:T(8,128)}, u32[]{:S(2)}, u32[]{:S(2)}) collective-permute-start(f32[256,512]{1,0:T(8,128)} %add.328), channel_id=1, source_target_pairs={{0,1},{1,2},{2,3},{3,0},{4,5},{5,6},{6,7},{7,4},{8,9},{9,10},{10,1... | collective-permute-start | bytes 1572872 | tf_op jit(solution)/shard_map/ppermute | solution.py:27
  516.6 24.3 %collective-permute-start.23 = (f32[256,512]{1,0:T(8,128)}, f32[256,512]{1,0:T(8,128)}, u32[]{:S(2)}, u32[]{:S(2)}) collective-permute-start(f32[256,512]{1,0:T(8,128)} %add.328), channel_id=1, source_target_pairs={{1,0},{2,1},{3,2},{0,3},{5,4},{6,5},{7,6},{4,7},{9,8},{10,9},{11,1... | collective-permute-start | bytes 1572872 | tf_op jit(solution)/shard_map/ppermute | solution.py:31
  533.4 20.0 %collective-permute-start.22 = (f32[256,512]{1,0:T(8,128)}, f32[256,512]{1,0:T(8,128)}, u32[]{:S(2)}, u32[]{:S(2)}) collective-permute-start(f32[256,512]{1,0:T(8,128)} %collective-permute-done.21), channel_id=1, source_target_pairs={{0,1},{1,2},{2,3},{3,0},{4,5},{5,6},{6,7},{7,4},{8,9},{9,10},{10,1... | collective-permute-start | bytes 1572872 | tf_op jit(solution)/shard_map/ppermute | solution.py:27
  574.4 14.0 %collective-permute-start.25 = (f32[256,512]{1,0:T(8,128)S(1)}, f32[256,512]{1,0:T(8,128)S(1)}, u32[]{:S(2)}, u32[]{:S(2)}) collective-permute-start(f32[256,512]{1,0:T(8,128)S(1)} %add.331), channel_id=1, source_target_pairs={{0,8},{8,0},{4,12},{12,4},{16,24},{24,16},{20,28},{28,20},{1,9},{9... | collective-permute-start | bytes 1572872 | tf_op jit(solution)/shard_map/ppermute | solution.py:50
  589.4 166.4 %all-gather.9.cloned.1.call-start = ((), (), s32[]{:S(2)}) async-start(), calls=%async_computation.24 | async-start | bytes 2621440 | tf_op jit(solution)/shard_map/all_gather | solution.py:190
  637.9 14.0 %collective-permute-start.27 = (f32[256,512]{1,0:T(8,128)S(1)}, f32[256,512]{1,0:T(8,128)S(1)}, u32[]{:S(2)}, u32[]{:S(2)}) collective-permute-start(f32[256,512]{1,0:T(8,128)S(1)} %add.333), channel_id=1, source_target_pairs={{0,8},{8,0},{4,12},{12,4},{16,24},{24,16},{20,28},{28,20},{1,9},{9... | collective-permute-start | bytes 1572872 | tf_op jit(solution)/shard_map/ppermute | solution.py:50
  652.0 16.6 %collective-permute-start.28 = (f32[256,512]{1,0:T(8,128)S(1)}, f32[256,512]{1,0:T(8,128)S(1)}, u32[]{:S(2)}, u32[]{:S(2)}) collective-permute-start(f32[256,512]{1,0:T(8,128)S(1)} %add.334), channel_id=1, source_target_pairs={{0,1},{1,2},{2,3},{3,0},{4,5},{5,6},{6,7},{7,4},{8,9},{9,10},{10,1... | collective-permute-start | bytes 1572872 | tf_op jit(solution)/shard_map/ppermute | solution.py:27
  652.2 24.2 %collective-permute-start.30 = (f32[256,512]{1,0:T(8,128)S(1)}, f32[256,512]{1,0:T(8,128)S(1)}, u32[]{:S(2)}, u32[]{:S(2)}) collective-permute-start(f32[256,512]{1,0:T(8,128)S(1)} %add.334), channel_id=1, source_target_pairs={{1,0},{2,1},{3,2},{0,3},{5,4},{6,5},{7,6},{4,7},{9,8},{10,9},{11,1... | collective-permute-start | bytes 1572872 | tf_op jit(solution)/shard_map/ppermute | solution.py:31
  668.6 20.8 %collective-permute-start.29 = (f32[256,512]{1,0:T(8,128)S(1)}, f32[256,512]{1,0:T(8,128)S(1)}, u32[]{:S(2)}, u32[]{:S(2)}) collective-permute-start(f32[256,512]{1,0:T(8,128)S(1)} %collective-permute-done.28), channel_id=1, source_target_pairs={{0,1},{1,2},{2,3},{3,0},{4,5},{5,6},{6,7},{7,4},{8,9},{9,10},{10,1... | collective-permute-start | bytes 1572872 | tf_op jit(solution)/shard_map/ppermute | solution.py:27
  711.8 154.5 %all-gather.11.cloned.1.call-start = ((), (), s32[]{:S(2)}) async-start(), calls=%async_computation.25 | async-start | bytes 2621440 | tf_op jit(solution)/shard_map/all_gather | solution.py:190
  761.0 16.7 %collective-permute-start.33 = (f32[256,512]{1,0:T(8,128)S(1)}, f32[256,512]{1,0:T(8,128)S(1)}, u32[]{:S(2)}, u32[]{:S(2)}) collective-permute-start(f32[256,512]{1,0:T(8,128)S(1)} %add.338), channel_id=1, source_target_pairs={{0,1},{1,2},{2,3},{3,0},{4,5},{5,6},{6,7},{7,4},{8,9},{9,10},{10,1... | collective-permute-start | bytes 1572872 | tf_op jit(solution)/shard_map/ppermute | solution.py:27
  761.2 25.1 %collective-permute-start.35 = (f32[256,512]{1,0:T(8,128)S(1)}, f32[256,512]{1,0:T(8,128)S(1)}, u32[]{:S(2)}, u32[]{:S(2)}) collective-permute-start(f32[256,512]{1,0:T(8,128)S(1)} %add.338), channel_id=1, source_target_pairs={{1,0},{2,1},{3,2},{0,3},{5,4},{6,5},{7,6},{4,7},{9,8},{10,9},{11,1... | collective-permute-start | bytes 1572872 | tf_op jit(solution)/shard_map/ppermute | solution.py:31
  777.7 21.6 %collective-permute-start.34 = (f32[256,512]{1,0:T(8,128)S(1)}, f32[256,512]{1,0:T(8,128)S(1)}, u32[]{:S(2)}, u32[]{:S(2)}) collective-permute-start(f32[256,512]{1,0:T(8,128)S(1)} %collective-permute-done.33), channel_id=1, source_target_pairs={{0,1},{1,2},{2,3},{3,0},{4,5},{5,6},{6,7},{7,4},{8,9},{9,10},{10,1... | collective-permute-start | bytes 1572872 | tf_op jit(solution)/shard_map/ppermute | solution.py:27
  872.8 16.7 %collective-permute-start.36 = (f32[256,512]{1,0:T(8,128)S(1)}, f32[256,512]{1,0:T(8,128)S(1)}, u32[]{:S(2)}, u32[]{:S(2)}) collective-permute-start(f32[256,512]{1,0:T(8,128)S(1)} %fusion), channel_id=1, source_target_pairs={{0,1},{1,2},{2,3},{3,0},{4,5},{5,6},{6,7},{7,4},{8,9},{9,10},{10,1... | collective-permute-start | bytes 1572872 | tf_op jit(solution)/shard_map/ppermute | solution.py:27
  873.0 24.7 %collective-permute-start.38 = (f32[256,512]{1,0:T(8,128)S(1)}, f32[256,512]{1,0:T(8,128)}, u32[]{:S(2)}, u32[]{:S(2)}) collective-permute-start(f32[256,512]{1,0:T(8,128)S(1)} %fusion), channel_id=1, source_target_pairs={{1,0},{2,1},{3,2},{0,3},{5,4},{6,5},{7,6},{4,7},{9,8},{10,9},{11,1... | collective-permute-start | bytes 1572872 | tf_op jit(solution)/shard_map/ppermute | solution.py:31
  889.4 21.3 %collective-permute-start.37 = (f32[256,512]{1,0:T(8,128)S(1)}, f32[256,512]{1,0:T(8,128)}, u32[]{:S(2)}, u32[]{:S(2)}) collective-permute-start(f32[256,512]{1,0:T(8,128)S(1)} %collective-permute-done.36), channel_id=1, source_target_pairs={{0,1},{1,2},{2,3},{3,0},{4,5},{5,6},{6,7},{7,4},{8,9},{9,10},{10,1... | collective-permute-start | bytes 1572872 | tf_op jit(solution)/shard_map/ppermute | solution.py:27
  (42 other events, 460.1 us)
Sparse Core Ops, SparseCore 0:
  38.5 42.7 reduce-scatter.7
  103.1 25.9 reduce-scatter.9
  156.7 26.3 reduce-scatter.11
  206.1 20.9 reduce-scatter.13
  266.4 20.8 reduce-scatter.15
  317.3 18.9 reduce-scatter.17
  386.6 19.0 reduce-scatter.19
  439.7 44.7 all-gather.4
  589.5 43.7 all-gather.6
  711.9 43.7 all-gather.8
  822.5 43.7 all-gather.10
